TPU v7x, 32 devices: a whole 2x2x4 slice. The times are simulated.
32 devices in a mesh: row: 4 (over z), col: 8 (over y, x, core).
Axes of the slice: x: 2, y: 2, z: 4, core: 2. Of those that a mesh axis runs over, the one named last changes fastest.
Arguments:
- tokens: bfloat16 [2048, 8192], P('row', 'col'), may hold values from -6 to 6
- weight: bfloat16 [8192, 26624], P('row', 'col'), may hold values from -0.0625 to 0.0625
- out_grad: bfloat16 [2048, 26624], P('row', 'col'), may hold values from -6 to 6
Outputs:
- preact: bfloat16 [2048, 26624], P('row', 'col')
- input_grad: bfloat16 [2048, 8192], P('row', 'col')
All inputs are finite; a program needn't handle non-finite values.
Results may differ from a plain program's by a relative error of at most 0.0049.
Values may be sent and summed in bfloat16 or wider, within the bound.
A program may use at most 192 MiB of HBM per device.

v0:
```python
import functools
import math

import jax
import jax.numpy as jnp
from jax import lax
from jax.experimental import pallas as pl
from jax.experimental.pallas import tpu as pltpu
from jax.sharding import PartitionSpec as P

sqrt_half = 1.0 / math.sqrt(2.0)
inv_root_tau = 1.0 / math.sqrt(2.0 * math.pi)

MESH = pl.DeviceIdType.MESH
CHUNKS = 4
WIDTH = 256
LAG = 1
OUT_SLOTS = 3


def gelu_slope(values):
    return (
        0.5 * (1.0 + lax.erf(values * sqrt_half))
        + values * jnp.exp(-0.5 * values * values) * inv_root_tau
    )


class Plan:
    def __init__(self, rows, cols, tokens, weight):
        self.rows, self.cols = rows, cols
        self.count, self.share = tokens.shape
        self.features, self.hidden = weight.shape
        self.ratio = self.features // self.share
        self.chips = cols // 2
        self.chunks = CHUNKS
        self.size = self.count // CHUNKS
        self.piece = self.size // cols
        self.width = WIDTH
        self.slices = self.hidden // WIDTH
        self.units = self.chunks * self.slices
        self.far = rows - 1
        self.slope_lag = self.far * LAG
        self.down_lag = 2 * self.far * LAG
        self.hold = self.slope_lag + 1
        self.in_slots = rows * LAG + 2
        self.grad_slots = rows * LAG + 3

    def scratch(self):
        bf, f4 = jnp.bfloat16, jnp.float32
        r, c, n, s, d = self.rows, self.cols, self.chunks, self.size, self.features
        far, w, piece, chips = self.far, self.width, self.piece, self.chips
        dma = pltpu.SemaphoreType.DMA
        return dict(
            a1=pltpu.VMEM((n, r, piece, d), bf),
            a2=pltpu.VMEM((n, r, piece, d), bf),
            tok=pltpu.VMEM((n, r, c, piece, d), bf),
            wv=pltpu.VMEM((self.slices, d, w), bf),
            part=pltpu.VMEM((self.hold, r * s, w), f4),
            rin=pltpu.VMEM((self.in_slots, 2, far, s, w), bf),
            rout=pltpu.VMEM((OUT_SLOTS, 2, far, s, w), bf),
            grad=pltpu.VMEM((self.grad_slots, r, s, w), bf),
            og=pltpu.VMEM((2, s, w), bf),
            pre=pltpu.VMEM((2, s, w), bf),
            acc=pltpu.VMEM((2, r, c, piece, d), f4),
            x_out=pltpu.VMEM((chips, r, piece, d), bf),
            x_in=pltpu.VMEM((2, chips, r, piece, d), bf),
            y_out=pltpu.VMEM((chips, r, piece, d), bf),
            y_in=pltpu.VMEM((2, chips, r, piece, d), bf),
            t_out=pltpu.VMEM((r, piece, d), bf),
            t_in=pltpu.VMEM((2, r, piece, d), bf),
            w_sem=dma((self.slices,)),
            s1s=dma((n, c)),
            s1r=dma((n, c)),
            s2s=dma((n, r)),
            s2r=dma((n, r)),
            s3s=dma((n, chips + 1)),
            s3r=dma((n, chips + 1)),
            s4s=dma((n, chips)),
            s4r=dma((n, chips)),
            rss=dma((OUT_SLOTS, 2, far)),
            rsr=dma((self.in_slots, 2, far)),
            ags=dma((self.grad_slots, 2, far)),
            agr=dma((self.grad_slots, 2, far)),
            og_sem=dma((2,)),
            pre_sem=dma((2,)),
            d1s=dma((chips,)),
            d1r=dma((2, chips)),
            d2s=dma((chips,)),
            d2r=dma((2, chips)),
            d3s=dma((r,)),
            d3r=dma((2, r)),
            d4s=dma((c,)),
            d4r=dma((n, c)),
        )


def aligned(index, size):
    return pl.ds(pl.multiple_of(index * size, size), size)


def body(pn, names, tokens, weight, out_grad, preact, input_grad, *refs):
    b = dict(zip(names, refs))
    rows, cols, chips, far = pn.rows, pn.cols, pn.chips, pn.far
    size, piece, width, share = pn.size, pn.piece, pn.width, pn.share
    units, slices, ratio = pn.units, pn.slices, pn.ratio
    r, c = lax.axis_index("row"), lax.axis_index("col")
    core, chip = c % 2, c // 2
    partner = c + 1 - 2 * core

    def remote(src, dst, send, recv, to):
        return pltpu.make_async_remote_copy(
            src_ref=src, dst_ref=dst, send_sem=send, recv_sem=recv, device_id=to, device_id_type=MESH
        )

    barrier = pltpu.get_barrier_semaphore()
    for j in range(1, rows):
        pl.semaphore_signal(barrier, inc=1, device_id=((r + j) % rows, c), device_id_type=MESH)
    for j in range(1, cols):
        pl.semaphore_signal(barrier, inc=1, device_id=(r, (c + j) % cols), device_id_type=MESH)
    pl.semaphore_wait(barrier, rows + cols - 2)

    def spread(k, j):
        to = (c + j) % cols
        src = tokens.at[aligned(k * cols + to, piece), :]
        dst = b["a1"].at[k, c // ratio, :, aligned(c % ratio, share)]
        if not j:
            return pltpu.make_async_copy(src, dst, b["s1s"].at[k, 0])
        return remote(src, dst, b["s1s"].at[k, j], b["s1r"].at[k, j], (r, to))

    def exchange(k, j):
        to = (r + j) % rows
        src, dst = b["a1"].at[k, to], b["a2"].at[k, r]
        if not j:
            return pltpu.make_async_copy(src, dst, b["s2s"].at[k, 0])
        return remote(src, dst, b["s2s"].at[k, j], b["s2r"].at[k, j], (to, c))

    def gather(k, j):
        src, dst = b["a2"].at[k], b["tok"].at[k, :, c]
        if not j:
            return pltpu.make_async_copy(src, dst, b["s3s"].at[k, 0])
        to = partner if j == chips else ((chip + j) % chips) * 2 + core
        return remote(src, dst, b["s3s"].at[k, j], b["s3r"].at[k, j], (r, to))

    def pass_on(k, j):
        here = b["tok"].at[k, :, ((chip - j + chips) % chips) * 2 + core]
        return remote(here, here, b["s4s"].at[k, j], b["s4r"].at[k, j], (r, partner))

    def begin(copy, k, number):
        for j in range(1, number):
            copy(k, j).start()
        copy(k, 0).start()

    def finish(copy, k, number):
        copy(k, 0).wait()
        for j in range(1, number):
            copy(k, j).wait_recv()
        for j in range(1, number):
            copy(k, j).wait_send()

    def stage1(k):
        begin(spread, k, cols)

    def stage2(k):
        finish(spread, k, cols)
        begin(exchange, k, rows)

    def stage3(k):
        finish(exchange, k, rows)
        begin(gather, k, chips + 1)

    def stage4(k):
        for j in range(1, chips):
            gather(k, j).wait_recv()
            pass_on(k, j).start()

    def stage5(k):
        gather(k, 0).wait()
        gather(k, chips).wait_recv()
        for j in range(1, chips + 1):
            gather(k, j).wait_send()
        for j in range(1, chips):
            pass_on(k, j).wait()

    def w_copy(g):
        return pltpu.make_async_copy(
            weight.at[:, aligned(g, width)], b["wv"].at[g], b["w_sem"].at[g]
        )

    stage1(0)

    @pl.loop(0, slices)
    def _(g):
        w_copy(g).start()

    stage2(0)
    stage3(0)
    stage4(0)

    def place(v):
        return aligned(v // slices, size), aligned(v % slices, width)

    def up(v):
        k, g = v // slices, v % slices

        @pl.when(g == 0)
        def _():
            stage5(k)

        @pl.when(k == 0)
        def _():
            w_copy(g).wait()

        b["part"][v % pn.hold] = jnp.dot(
            b["tok"][k].reshape(rows * size, pn.features),
            b["wv"][g],
            preferred_element_type=jnp.float32,
        )

    def towards(way):
        return r if way == 0 else far - r

    def sum_copy(v, way, h):
        slot = v % OUT_SLOTS
        return remote(
            b["rout"].at[slot, way, h],
            b["rin"].at[v % pn.in_slots, way, h],
            b["rss"].at[slot, way, h],
            b["rsr"].at[v % pn.in_slots, way, h],
            ((r + 1) % rows if way == 0 else (r + far) % rows, c),
        )

    def sums(v, h):
        for way in (0, 1):
            pos = towards(way)

            @pl.when(pos <= h)
            def _(way=way, pos=pos):
                @pl.when(v >= OUT_SLOTS)
                def _():
                    sum_copy(v, way, h).wait_send()

                owner = pos + far - h
                owner = owner if way == 0 else far - owner
                mine = b["part"].at[v % pn.hold, aligned(owner, size), :]
                out = b["rout"].at[v % OUT_SLOTS, way, h]

                @pl.when(pos == 0)
                def _():
                    out[...] = mine[...].astype(jnp.bfloat16)

                if h:

                    @pl.when(pos > 0)
                    def _():
                        sum_copy(v, way, h - 1).wait_recv()
                        got = b["rin"][v % pn.in_slots, way, h - 1]
                        out[...] = (got.astype(jnp.float32) + mine[...]).astype(jnp.bfloat16)

                sum_copy(v, way, h).start()

    def og_copy(v):
        return pltpu.make_async_copy(out_grad.at[place(v)], b["og"].at[v % 2], b["og_sem"].at[v % 2])

    def pre_copy(v):
        return pltpu.make_async_copy(b["pre"].at[v % 2], preact.at[place(v)], b["pre_sem"].at[v % 2])

    def grad_copy(v, way, h):
        slot = v % pn.grad_slots
        source = lax.rem(r + (rows - h if way == 0 else h), rows)
        block = b["grad"].at[slot, source]
        return remote(
            block,
            block,
            b["ags"].at[slot, way, h],
            b["agr"].at[slot, way, h],
            ((r + 1) % rows if way == 0 else (r + far) % rows, c),
        )

    def slope(v):
        mine = b["part"].at[v % pn.hold, aligned(r, size), :]
        for way in (0, 1):

            @pl.when(towards(way) > 0)
            def _(way=way):
                sum_copy(v, way, far - 1).wait_recv()
                mine[...] += b["rin"][v % pn.in_slots, way, far - 1].astype(jnp.float32)

        og_copy(v).wait()

        @pl.when(v >= 2)
        def _():
            pre_copy(v).wait()

        full_pre = mine[...]
        gradient = b["og"][v % 2].astype(jnp.float32) * gelu_slope(full_pre)
        b["grad"][v % pn.grad_slots, r] = gradient.astype(jnp.bfloat16)
        for way in (0, 1):

            @pl.when(towards(way) < far)
            def _(way=way):
                grad_copy(v, way, 0).start()

        b["pre"][v % 2] = full_pre.astype(jnp.bfloat16)
        pre_copy(v).start()

        @pl.when(v + 1 < units)
        def _():
            og_copy(v + 1).start()

    def grads(v, h):
        for way in (0, 1):

            @pl.when(towards(way) >= h)
            def _(way=way):
                grad_copy(v, way, h - 1).wait_recv()

                @pl.when(towards(way) < far)
                def _():
                    grad_copy(v, way, h).start()

    def down(v):
        k, g = v // slices, v % slices
        for way in (0, 1):

            @pl.when(towards(way) == far)
            def _(way=way):
                grad_copy(v, way, far - 1).wait_recv()

        acc = b["acc"].at[k % 2]

        @pl.when(g == 0)
        def _():
            acc[...] = jnp.zeros_like(acc)

        step = min(512, pn.features)
        blocks = b["grad"][v % pn.grad_slots].reshape(rows * size, width)
        for n in range(pn.features // step):
            part = lax.dot_general(
                blocks,
                b["wv"][g, n * step : (n + 1) * step],
                (((1,), (1,)), ((), ())),
                preferred_element_type=jnp.float32,
            )
            acc[:, :, :, n * step : (n + 1) * step] += part.reshape(rows, cols, piece, step)
        for way in (0, 1):
            for h in range(far):

                @pl.when((towards(way) >= h) & (towards(way) < far))
                def _(way=way, h=h):
                    grad_copy(v, way, h).wait_send()

    def pair_copy(k, q):
        return remote(
            b["x_out"].at[q], b["x_in"].at[k % 2, q], b["d1s"].at[q], b["d1r"].at[k % 2, q], (r, partner)
        )

    def plane_copy(k, j):
        to = ((chip + j) % chips) * 2 + core
        return remote(
            b["y_out"].at[j], b["y_in"].at[k % 2, j], b["d2s"].at[j], b["d2r"].at[k % 2, j], (r, to)
        )

    def row_copy(k, j):
        to = (r + j) % rows
        src, dst = b["t_out"].at[to], b["t_in"].at[k % 2, r]
        if not j:
            return pltpu.make_async_copy(src, dst, b["d3s"].at[0])
        return remote(src, dst, b["d3s"].at[j], b["d3r"].at[k % 2, j], (to, c))

    def owner_copy(k, j):
        to = (c + j) % cols
        src = b["t_in"].at[k % 2, to // ratio, :, aligned(to % ratio, share)]
        dst = input_grad.at[aligned(k * cols + c, piece), :]
        if not j:
            return pltpu.make_async_copy(src, dst, b["d4s"].at[0])
        return remote(src, dst, b["d4s"].at[j], b["d4r"].at[k, j], (r, to))

    def pair(k):
        for q in range(chips):

            @pl.when(k > 0)
            def _(q=q):
                pair_copy(k, q).wait_send()

            b["x_out"][q] = b["acc"][k % 2, :, q * 2 + 1 - core].astype(jnp.bfloat16)
            pair_copy(k, q).start()

    def plane(k):
        for q in range(chips):
            pair_copy(k, q).wait_recv()
        for j in list(range(1, chips)) + [0]:
            q = (chip + j) % chips
            total = b["acc"][k % 2, :, q * 2 + core] + b["x_in"][k % 2, q].astype(jnp.float32)
            if j:

                @pl.when(k > 0)
                def _(j=j):
                    plane_copy(k, j).wait_send()

                b["y_out"][j] = total.astype(jnp.bfloat16)
                plane_copy(k, j).start()
            else:
                b["acc"][k % 2, :, q * 2 + core] = total

    def owners_wait():
        for j in range(1, cols):
            owner_copy(0, j).wait_send()
        owner_copy(0, 0).wait()

    def exchange_back(k):
        @pl.when(k > 0)
        def _():
            owners_wait()
            for j in range(1, rows):
                row_copy(k, j).wait_send()

        total = b["acc"][k % 2, :, c]
        for j in range(1, chips):
            plane_copy(k, j).wait_recv()
            total = total + b["y_in"][k % 2, j].astype(jnp.float32)
        b["t_out"][...] = total.astype(jnp.bfloat16)
        for j in range(1, rows):
            row_copy(k, j).start()
        row_copy(k, 0).start()

    def owners(k):
        row_copy(k, 0).wait()
        for j in range(1, rows):
            row_copy(k, j).wait_recv()
        for j in range(1, cols):
            owner_copy(k, j).start()
        owner_copy(k, 0).start()

    def in_range(v):
        return (v >= 0) & (v < units)

    def at_chunk_end(v, action):
        @pl.when(in_range(v) & (v % slices == slices - 1))
        def _():
            action(v // slices)

    og_copy(0).start()
    ends = (0, 1, 3, 5)

    @pl.loop(0, units + pn.down_lag + ends[-1] + 1)
    def _(i):
        @pl.when(i < units)
        def _():
            up(i)

        for h in range(far):
            v = i - h * LAG

            @pl.when(in_range(v))
            def _(v=v, h=h):
                sums(v, h)

        @pl.when(in_range(i - pn.slope_lag))
        def _():
            slope(i - pn.slope_lag)

        for h in range(1, far):
            v = i - pn.slope_lag - h * LAG

            @pl.when(in_range(v))
            def _(v=v, h=h):
                grads(v, h)

        @pl.when(in_range(i - pn.down_lag))
        def _():
            down(i - pn.down_lag)

        for lag, action in zip(ends, (pair, plane, exchange_back, owners)):
            at_chunk_end(i - pn.down_lag - lag, action)

        for at, action in enumerate((stage1, stage2, stage3, stage4)):

            @pl.when((i < units - slices) & (i % slices == at * slices // 4))
            def _(action=action):
                action(i // slices + 1)

    for back in range(1, OUT_SLOTS + 1):
        for way in (0, 1):
            for h in range(far):

                @pl.when(towards(way) <= h)
                def _(back=back, way=way, h=h):
                    sum_copy(units - back, way, h).wait_send()

    for v in (units - 2, units - 1):
        pre_copy(v).wait()
    last = pn.chunks - 1
    for q in range(chips):
        pair_copy(last, q).wait_send()
    for j in range(1, chips):
        plane_copy(last, j).wait_send()
    for j in range(1, rows):
        row_copy(last, j).wait_send()
    owners_wait()

    @pl.loop(0, pn.chunks)
    def _(k):
        for j in range(1, cols):
            owner_copy(k, j).wait_recv()


def per_device(rows, cols, tokens, weight, out_grad):
    pn = Plan(rows, cols, tokens, weight)
    scratch = pn.scratch()
    anywhere = pl.BlockSpec(memory_space=pl.ANY)
    flops = 4 * pn.count * rows * pn.features * pn.hidden
    return pl.pallas_call(
        functools.partial(body, pn, tuple(scratch)),
        out_shape=(
            jax.ShapeDtypeStruct(out_grad.shape, jnp.bfloat16),
            jax.ShapeDtypeStruct(tokens.shape, jnp.bfloat16),
        ),
        in_specs=[anywhere] * 3,
        out_specs=(anywhere, anywhere),
        scratch_shapes=list(scratch.values()),
        compiler_params=pltpu.CompilerParams(
            collective_id=0, has_side_effects=True, vmem_limit_bytes=62 * 2**20
        ),
        cost_estimate=pl.CostEstimate(flops=flops, bytes_accessed=2 * weight.size, transcendentals=0),
    )(tokens, weight, out_grad)


def solution(mesh):
    rows, cols = mesh.shape["row"], mesh.shape["col"]
    return jax.shard_map(
        functools.partial(per_device, rows, cols),
        mesh=mesh,
        in_specs=(P("row", "col"), P("row", "col"), P("row", "col")),
        out_specs=(P("row", "col"), P("row", "col")),
        check_vma=False,
    )
```

profile of v0, /device:TPU:0, one launch (start us, length us, event | category | flops | bytes accessed | tf_op | source)
XLA Modules:
  0.0 402.6 jit_solution(6688314085692330482)
XLA Ops:
  0.6 396.9 %shard_map.50 = (bf16[512,3328]{1,0:T(8,128)(2,1)}, bf16[512,1024]{1,0:T(8,128)(2,1)}) custom-call(bf16[512,1024]{1,0:T(8,128)(2,1)} %tokens.1, bf16[2048,3328]{1,0:T(8,128)(2,1)} %weight.1, bf16[512,3328]{1,0:T(8,128)(2,1)} %out_grad.1), custom_call_target="tpu_custom_call" | custom-call | flops 55834574848 | bytes 13631488 | tf_op jit(solution)/shard_map/pallas_call | solution.py:512
  397.6 0.0 copy-start
  397.6 4.0 copy.7
  401.6 0.0 copy-done
  401.6 1.0 copy.8
Async XLA Ops:
  397.6 4.0 %copy-start = (bf16[512,1024]{1,0:T(8,128)(2,1)S(1)}, bf16[512,1024]{1,0:T(8,128)(2,1)}, u32[]{:S(2)}) copy-start(bf16[512,1024]{1,0:T(8,128)(2,1)} %get-tuple-element.5) | copy-start | bytes 3145732
where the time goes:
time: 403 us
  Pallas kernels  397 us (99%)
  local copies, waits for them, and re-layouts  4.99 us (1%)
    pallas_call x1, Pallas kernels, per_device(): pl.pallas_call(functools.partial(body, pn, tuple(scratch)), out_shape=(ja...  397 us

commit v1 on v0

v1 whole, which is shorter than its diff:
```python
import functools
import math

import jax
import jax.numpy as jnp
from jax import lax
from jax.experimental import pallas as pl
from jax.experimental.pallas import tpu as pltpu
from jax.sharding import PartitionSpec as P

sqrt_half = 1.0 / math.sqrt(2.0)
inv_root_tau = 1.0 / math.sqrt(2.0 * math.pi)

MESH = pl.DeviceIdType.MESH
CHUNKS = 8
WIDTH = 256
LAG = 2
OUT_SLOTS = 3
AHEAD = 4


def gelu_slope(values):
    return (
        0.5 * (1.0 + lax.erf(values * sqrt_half))
        + values * jnp.exp(-0.5 * values * values) * inv_root_tau
    )


class Plan:
    def __init__(self, rows, cols, tokens, weight):
        self.rows, self.cols = rows, cols
        self.count, self.share = tokens.shape
        self.features, self.hidden = weight.shape
        self.ratio = self.features // self.share
        self.chips = cols // 2
        self.chunks = CHUNKS
        self.size = self.count // CHUNKS
        self.thin = max(self.share // cols, min(self.share, 128))
        self.across = self.share // self.thin
        self.deep = cols // self.across
        self.short = self.size // self.deep
        self.piece = self.ratio * self.thin
        self.width = WIDTH if self.hidden % WIDTH == 0 else 128
        self.slices = self.hidden // self.width
        assert self.deep * self.short * CHUNKS == self.count and self.slices * self.width == self.hidden
        self.units = self.chunks * self.slices
        self.far = rows - 1
        self.lag = LAG if rows <= 4 else 1
        self.ahead = min(AHEAD, self.chunks)
        self.slope_lag = self.far * self.lag
        self.down_lag = 2 * self.far * self.lag
        self.hold = self.slope_lag + 1
        self.in_slots = rows * self.lag + 2
        self.grad_slots = rows * self.lag + 3

    def scratch(self):
        bf, f4 = jnp.bfloat16, jnp.float32
        r, c, n, s, d = self.rows, self.cols, self.chunks, self.size, self.features
        far, w, piece, chips = self.far, self.width, self.piece, self.chips
        low = self.short
        dma = pltpu.SemaphoreType.DMA
        return dict(
            a1=pltpu.VMEM((n, r, low, piece), bf),
            a2=pltpu.VMEM((n, r, low, piece), bf),
            tok=pltpu.VMEM((n, r, s, d), bf),
            wv=pltpu.VMEM((self.slices, self.across, self.ratio, self.thin, w), bf),
            part=pltpu.VMEM((self.hold, r * s, w), f4),
            rin=pltpu.VMEM((self.in_slots, 2, far, s, w), bf),
            rout=pltpu.VMEM((OUT_SLOTS, 2, far, s, w), bf),
            grad=pltpu.VMEM((self.grad_slots, r, s, w), bf),
            og=pltpu.VMEM((2, s, w), bf),
            pre=pltpu.VMEM((2, s, w), bf),
            acc=pltpu.VMEM((2, self.across, r, s, piece), f4),
            x_out=pltpu.VMEM((chips, r, low, piece), bf),
            x_in=pltpu.VMEM((2, chips, r, low, piece), bf),
            y_out=pltpu.VMEM((chips, r, low, piece), bf),
            y_in=pltpu.VMEM((2, chips, r, low, piece), bf),
            t_out=pltpu.VMEM((r, low, piece), bf),
            t_in=pltpu.VMEM((2, r, low, piece), bf),
            w_sem=dma((self.slices, self.ratio)),
            s1s=dma((n, c)),
            s1r=dma((n, c)),
            s2s=dma((n, r)),
            s2r=dma((n, r)),
            s3s=dma((2, r, chips + 1)),
            s3r=dma((2, r, chips + 1)),
            s4s=dma((2, r, chips)),
            s4r=dma((2, r, chips)),
            rss=dma((OUT_SLOTS, 2, far)),
            rsr=dma((self.in_slots, 2, far)),
            ags=dma((self.grad_slots, 2, far)),
            agr=dma((self.grad_slots, 2, far)),
            og_sem=dma((2,)),
            pre_sem=dma((2,)),
            d1s=dma((chips,)),
            d1r=dma((2, chips)),
            d2s=dma((chips, r)),
            d2r=dma((2, chips, r)),
            d3s=dma((r,)),
            d3r=dma((2, r)),
            d4s=dma((c,)),
            d4r=dma((n, c)),
        )


def aligned(index, size):
    return pl.ds(pl.multiple_of(index * size, size), size)


def body(pn, names, tokens, weight, out_grad, preact, input_grad, *refs):
    b = dict(zip(names, refs))
    rows, cols, chips, far = pn.rows, pn.cols, pn.chips, pn.far
    size, piece, width, thin = pn.size, pn.piece, pn.width, pn.thin
    units, slices, ratio = pn.units, pn.slices, pn.ratio
    r, c = lax.axis_index("row"), lax.axis_index("col")
    core, chip = c % 2, c // 2
    partner = c + 1 - 2 * core
    across, deep, short = pn.across, pn.deep, pn.short

    def tall(q):
        return (q // across if deep > 1 else 0), (q % across if deep > 1 else q)


    def remote(src, dst, send, recv, to):
        return pltpu.make_async_remote_copy(
            src_ref=src, dst_ref=dst, send_sem=send, recv_sem=recv, device_id=to, device_id_type=MESH
        )

    barrier = pltpu.get_barrier_semaphore()
    for j in range(1, rows):
        pl.semaphore_signal(barrier, inc=1, device_id=((r + j) % rows, c), device_id_type=MESH)
    for j in range(1, cols):
        pl.semaphore_signal(barrier, inc=1, device_id=(r, (c + j) % cols), device_id_type=MESH)
    pl.semaphore_wait(barrier, rows + cols - 2)

    def others(action, far_first=False):
        steps = [s for d in range(1, rows) for s in (d, -d)]
        for s in steps[::-1] if far_first else steps:

            @pl.when((r + s >= 0) & (r + s < rows))
            def _(s=s):
                action(r + s)

    def spread(k, j):
        to = (c + j) % cols
        down_part, side = tall(to)
        src = tokens.at[aligned(k * deep + down_part, short), aligned(side, thin)]
        dst = b["a1"].at[k, c // ratio, :, aligned(c % ratio, thin)]
        if not j:
            return pltpu.make_async_copy(src, dst, b["s1s"].at[k, 0])
        return remote(src, dst, b["s1s"].at[k, j], b["s1r"].at[k, j], (r, to))

    def exchange(k, to):
        return remote(
            b["a1"].at[k, to], b["a2"].at[k, r], b["s2s"].at[k, to], b["s2r"].at[k, r], (to, c)
        )

    def exchanged(k, source):
        return remote(
            b["a1"].at[k, r], b["a2"].at[k, source], b["s2s"].at[k, r], b["s2r"].at[k, source], (source, c)
        )

    def token_part(k, row, q):
        down_part, side = tall(q)
        return b["tok"].at[k, row, aligned(down_part, short), aligned(side, piece)]

    def gather(k, row, j, own=False):
        src = b["a1"].at[k, r] if own else b["a2"].at[k, row]
        dst = token_part(k, row, c)
        send = b["s3s"].at[k % 2, row, j]
        if not j:
            return pltpu.make_async_copy(src, dst, send)
        to = partner if j == chips else ((chip + j) % chips) * 2 + core
        return remote(src, dst, send, b["s3r"].at[k % 2, row, j], (r, to))

    def pass_on(k, row, j):
        here = token_part(k, row, ((chip - j + chips) % chips) * 2 + core)
        return remote(here, here, b["s4s"].at[k % 2, row, j], b["s4r"].at[k % 2, row, j], (r, partner))

    def stage1(k):
        for j in range(1, cols):
            spread(k, j).start()
        spread(k, 0).start()

    def stage2(k):
        spread(k, 0).wait()
        for j in range(1, cols):
            spread(k, j).wait_recv()
        others(lambda to: exchange(k, to).start(), far_first=True)
        for j in range(1, cols):
            spread(k, j).wait_send()

    def gather_row(k, row, own=False):
        for j in list(range(1, chips + 1)) + [0]:
            gather(k, row, j, own).start()

    def stage3(k, with_own=True):
        if with_own:
            gather_row(k, r, own=True)

        def action(row):
            exchanged(k, row).wait_recv()
            gather_row(k, row)

        others(action)

    def stage4(k):
        def action(row):
            for j in range(1, chips):
                gather(k, row, j).wait_recv()
                pass_on(k, row, j).start()

        action(r)
        others(action)

    def stage5(k):
        others(lambda to: exchange(k, to).wait_send())
        for row in range(rows):
            gather(k, row, 0).wait()
            gather(k, row, chips).wait_recv()
            for j in range(1, chips):
                pass_on(k, row, j).wait()
            for j in range(1, chips + 1):
                gather(k, row, j).wait_send()

    def w_copy(g, part):
        return pltpu.make_async_copy(
            weight.at[part, :, :, aligned(g, width)], b["wv"].at[g, :, part], b["w_sem"].at[g, part]
        )

    for k in range(pn.ahead):
        stage1(k)

    @pl.loop(0, slices)
    def _(g):
        for part in range(ratio):
            w_copy(g, part).start()

    stage2(0)
    gather_row(0, r, own=True)
    for k in range(1, pn.ahead):
        stage2(k)
    stage3(0, with_own=False)
    stage4(0)

    def place(v):
        return aligned(v // slices, size), aligned(v % slices, width)

    def up(v):
        k, g = v // slices, v % slices

        @pl.when(g == 0)
        def _():
            stage5(k)

        @pl.when(k == 0)
        def _():
            for part in range(ratio):
                w_copy(g, part).wait()

        b["part"][v % pn.hold] = jnp.dot(
            b["tok"][k].reshape(rows * size, pn.features),
            b["wv"][g].reshape(pn.features, width),
            preferred_element_type=jnp.float32,
        )

    def towards(way):
        return r if way == 0 else far - r

    def sum_copy(v, way, h):
        slot = v % OUT_SLOTS
        return remote(
            b["rout"].at[slot, way, h],
            b["rin"].at[v % pn.in_slots, way, h],
            b["rss"].at[slot, way, h],
            b["rsr"].at[v % pn.in_slots, way, h],
            ((r + 1) % rows if way == 0 else (r + far) % rows, c),
        )

    def sums(v, h):
        for way in (0, 1):
            pos = towards(way)

            @pl.when(pos <= h)
            def _(way=way, pos=pos):
                @pl.when(v >= OUT_SLOTS)
                def _():
                    sum_copy(v, way, h).wait_send()

                owner = pos + far - h
                owner = owner if way == 0 else far - owner
                mine = b["part"].at[v % pn.hold, aligned(owner, size), :]
                out = b["rout"].at[v % OUT_SLOTS, way, h]

                @pl.when(pos == 0)
                def _():
                    out[...] = mine[...].astype(jnp.bfloat16)

                if h:

                    @pl.when(pos > 0)
                    def _():
                        sum_copy(v, way, h - 1).wait_recv()
                        got = b["rin"][v % pn.in_slots, way, h - 1]
                        out[...] = (got.astype(jnp.float32) + mine[...]).astype(jnp.bfloat16)

                sum_copy(v, way, h).start()

    def og_copy(v):
        return pltpu.make_async_copy(out_grad.at[place(v)], b["og"].at[v % 2], b["og_sem"].at[v % 2])

    def pre_copy(v):
        return pltpu.make_async_copy(b["pre"].at[v % 2], preact.at[place(v)], b["pre_sem"].at[v % 2])

    def grad_copy(v, way, h):
        slot = v % pn.grad_slots
        source = lax.rem(r + (rows - h if way == 0 else h), rows)
        block = b["grad"].at[slot, source]
        return remote(
            block,
            block,
            b["ags"].at[slot, way, h],
            b["agr"].at[slot, way, h],
            ((r + 1) % rows if way == 0 else (r + far) % rows, c),
        )

    def slope(v):
        mine = b["part"].at[v % pn.hold, aligned(r, size), :]
        for way in (0, 1):

            @pl.when(towards(way) > 0)
            def _(way=way):
                sum_copy(v, way, far - 1).wait_recv()
                mine[...] += b["rin"][v % pn.in_slots, way, far - 1].astype(jnp.float32)

        og_copy(v).wait()

        @pl.when(v >= 2)
        def _():
            pre_copy(v).wait()

        full_pre = mine[...]
        gradient = b["og"][v % 2].astype(jnp.float32) * gelu_slope(full_pre)
        b["grad"][v % pn.grad_slots, r] = gradient.astype(jnp.bfloat16)
        for way in (0, 1):

            @pl.when(towards(way) < far)
            def _(way=way):
                grad_copy(v, way, 0).start()

        b["pre"][v % 2] = full_pre.astype(jnp.bfloat16)
        pre_copy(v).start()

        @pl.when(v + 1 < units)
        def _():
            og_copy(v + 1).start()

    def grads(v, h):
        for way in (0, 1):

            @pl.when(towards(way) >= h)
            def _(way=way):
                grad_copy(v, way, h - 1).wait_recv()

                @pl.when(towards(way) < far)
                def _():
                    grad_copy(v, way, h).start()

    def down(v):
        k, g = v // slices, v % slices
        for way in (0, 1):

            @pl.when(towards(way) == far)
            def _(way=way):
                grad_copy(v, way, far - 1).wait_recv()

        acc = b["acc"].at[k % 2]

        @pl.when(g == 0)
        def _():
            acc[...] = jnp.zeros_like(acc)

        group = max(1, min(512 // piece, across))
        blocks = b["grad"][v % pn.grad_slots].reshape(rows * size, width)
        for n in range(0, across, group):
            part = lax.dot_general(
                blocks,
                b["wv"][g, n : n + group].reshape(group * piece, width),
                (((1,), (1,)), ((), ())),
                preferred_element_type=jnp.float32,
            )
            for m in range(group):
                acc[n + m] += part[:, m * piece : (m + 1) * piece].reshape(rows, size, piece)
        for way in (0, 1):
            for h in range(far):

                @pl.when((towards(way) >= h) & (towards(way) < far))
                def _(way=way, h=h):
                    grad_copy(v, way, h).wait_send()

    def pair_copy(k, j):
        return remote(
            b["x_out"].at[j], b["x_in"].at[k % 2, j], b["d1s"].at[j], b["d1r"].at[k % 2, j], (r, partner)
        )

    def plane_copy(k, j, row):
        to = ((chip + j) % chips) * 2 + core
        return remote(
            b["y_out"].at[j, row],
            b["y_in"].at[k % 2, j, row],
            b["d2s"].at[j, row],
            b["d2r"].at[k % 2, j, row],
            (r, to),
        )

    def row_copy(k, to):
        return remote(
            b["t_out"].at[to], b["t_in"].at[k % 2, r], b["d3s"].at[to], b["d3r"].at[k % 2, r], (to, c)
        )

    def row_arrival(k, source):
        return remote(
            b["t_out"].at[r], b["t_in"].at[k % 2, source], b["d3s"].at[r], b["d3r"].at[k % 2, source], (source, c)
        )

    def owned(k, q):
        down_part, side = tall(q)
        return input_grad.at[aligned(k * deep + down_part, short), aligned(side, thin)]

    def acc_part(k, q, row=None):
        down_part, side = tall(q)
        rows_of = slice(None) if row is None else row
        return b["acc"][k % 2, side, rows_of, aligned(down_part, short)]

    def owner_copy(k, to, local=False):
        src = b["t_in"].at[k % 2, to // ratio, :, aligned(to % ratio, thin)]
        dst = owned(k, c)
        if local:
            return pltpu.make_async_copy(src, dst, b["d4s"].at[c])
        return remote(src, dst, b["d4s"].at[to], b["d4r"].at[k, c], (r, to))

    def owner_arrival(k, source):
        src = b["t_in"].at[0, 0, :, aligned(0, thin)]
        dst = owned(k, source)
        return remote(src, dst, b["d4s"].at[source], b["d4r"].at[k, source], (r, source))

    def pair(k):
        for j in list(range(1, chips)) + [0]:

            @pl.when(k > 0)
            def _(j=j):
                pair_copy(k, j).wait_send()

            q = (chip + j) % chips
            b["x_out"][j] = acc_part(k, q * 2 + 1 - core).astype(jnp.bfloat16)
            pair_copy(k, j).start()

    def plane(k):
        for j in range(chips):
            pair_copy(k, j).wait_recv()

        def action(row):
            for j in range(1, chips):
                q = (chip + j) % chips

                @pl.when(k > 0)
                def _(j=j):
                    plane_copy(k, j, row).wait_send()

                total = acc_part(k, q * 2 + core, row) + b["x_in"][k % 2, j, row].astype(jnp.float32)
                b["y_out"][j, row] = total.astype(jnp.bfloat16)
                plane_copy(k, j, row).start()

        others(action, far_first=True)
        action(r)

    def owners_wait():
        for j in range(1, cols):
            owner_copy(0, (c + j) % cols).wait_send()
        owner_copy(0, c, local=True).wait()

    def exchange_back(k):
        @pl.when(k > 0)
        def _():
            owners_wait()
            others(lambda to: row_copy(k, to).wait_send())

        def total(row):
            value = acc_part(k, c, row) + b["x_in"][k % 2, 0, row].astype(jnp.float32)
            for j in range(1, chips):
                plane_copy(k, j, row).wait_recv()
                value = value + b["y_in"][k % 2, j, row].astype(jnp.float32)
            return value.astype(jnp.bfloat16)

        def action(row):
            b["t_out"][row] = total(row)
            row_copy(k, row).start()

        others(action, far_first=True)
        b["t_in"][k % 2, r] = total(r)

    def owners(k):
        def action(row):
            for part in range(ratio):
                to = row * ratio + part

                @pl.when(to != c)
                def _(to=to):
                    owner_copy(k, to).start()

                @pl.when(to == c)
                def _():
                    owner_copy(k, c, local=True).start()

        def arrived(row):
            row_arrival(k, row).wait_recv()
            action(row)

        action(r)
        others(arrived)

    def in_range(v):
        return (v >= 0) & (v < units)

    def at_chunk_end(v, action):
        @pl.when(in_range(v) & (v % slices == slices - 1))
        def _():
            action(v // slices)

    og_copy(0).start()
    ends = (0, 1, slices // 3, 2 * slices // 3)

    @pl.loop(0, units + pn.down_lag + ends[-1] + 1)
    def _(i):
        @pl.when(i < units)
        def _():
            up(i)

        for h in range(far):
            v = i - h * pn.lag

            @pl.when(in_range(v))
            def _(v=v, h=h):
                sums(v, h)

        @pl.when(in_range(i - pn.slope_lag))
        def _():
            slope(i - pn.slope_lag)

        for h in range(1, far):
            v = i - pn.slope_lag - h * pn.lag

            @pl.when(in_range(v))
            def _(v=v, h=h):
                grads(v, h)

        @pl.when(in_range(i - pn.down_lag))
        def _():
            down(i - pn.down_lag)

        for lag, action in zip(ends, (pair, plane, exchange_back, owners)):
            at_chunk_end(i - pn.down_lag - lag, action)

        for at, (action, early) in enumerate(
            ((stage1, pn.ahead), (stage2, pn.ahead), (stage3, 1), (stage4, 1))
        ):

            @pl.when((i < units - early * slices) & (i % slices == at * slices // 4))
            def _(action=action, early=early):
                action(i // slices + early)

    for back in range(1, OUT_SLOTS + 1):
        for way in (0, 1):
            for h in range(far):

                @pl.when(towards(way) <= h)
                def _(back=back, way=way, h=h):
                    sum_copy(units - back, way, h).wait_send()

    for v in (units - 2, units - 1):
        pre_copy(v).wait()
    last = pn.chunks - 1
    for j in range(chips):
        pair_copy(last, j).wait_send()
    for j in range(1, chips):
        for row in range(rows):
            plane_copy(last, j, row).wait_send()
    others(lambda to: row_copy(last, to).wait_send())
    owners_wait()

    @pl.loop(0, pn.chunks)
    def _(k):
        for j in range(1, cols):
            owner_arrival(k, (c + j) % cols).wait_recv()


def per_device(rows, cols, tokens, weight, out_grad):
    pn = Plan(rows, cols, tokens, weight)
    scratch = pn.scratch()
    anywhere = pl.BlockSpec(memory_space=pl.ANY)
    flops = 4 * pn.count * rows * pn.features * pn.hidden
    return pl.pallas_call(
        functools.partial(body, pn, tuple(scratch)),
        out_shape=(
            jax.ShapeDtypeStruct(out_grad.shape, jnp.bfloat16),
            jax.ShapeDtypeStruct(tokens.shape, jnp.bfloat16),
        ),
        in_specs=[anywhere] * 3,
        out_specs=(anywhere, anywhere),
        scratch_shapes=list(scratch.values()),
        compiler_params=pltpu.CompilerParams(
            collective_id=0, has_side_effects=True, vmem_limit_bytes=62 * 2**20
        ),
        cost_estimate=pl.CostEstimate(flops=flops, bytes_accessed=2 * weight.size, transcendentals=0),
    )(tokens, weight.reshape(pn.ratio, pn.across, pn.thin, pn.hidden), out_grad)


def solution(mesh):
    rows, cols = mesh.shape["row"], mesh.shape["col"]
    return jax.shard_map(
        functools.partial(per_device, rows, cols),
        mesh=mesh,
        in_specs=(P("row", "col"), P("row", "col"), P("row", "col")),
        out_specs=(P("row", "col"), P("row", "col")),
        check_vma=False,
    )
```

time: 403 us -> 380 us (0.943)
  Pallas kernels: 397 us -> 374 us
    pallas_call x1, Pallas kernels: 397 us -> 374 us  [per_device(): pl.pallas_call(functools.partial(body, pn, tuple(scratch)), out_shape=(ja...]
where the time goes in v1:
time: 380 us
  Pallas kernels  374 us (98%)
  local copies, waits for them, and re-layouts  4.99 us (1%)
    pallas_call x1, Pallas kernels, per_device(): pl.pallas_call(functools.partial(body, pn, tuple(scratch)), out_shape=(ja...  374 us

profile of v1, /device:TPU:0, one launch (start us, length us, event | category | flops | bytes accessed | tf_op | source)
XLA Modules:
  0.0 379.6 jit_solution(17855750422224960973)
XLA Ops:
  0.6 374.0 %shard_map.50 = (bf16[512,3328]{1,0:T(8,128)(2,1)}, bf16[512,1024]{1,0:T(8,128)(2,1)}) custom-call(bf16[512,1024]{1,0:T(8,128)(2,1)} %tokens.1, bf16[2,8,128,3328]{3,2,1,0:T(8,128)(2,1)} %bitcast.1, bf16[512,3328]{1,0:T(8,128)(2,1)} %out_grad.1), custom_call_target="tpu_custom_call" | custom-call | flops 55834574848 | bytes 13631488 | tf_op jit(solution)/shard_map/pallas_call | solution.py:602
  374.6 0.0 copy-start
  374.6 4.0 %copy.7 = bf16[512,3328]{1,0:T(8,128)(2,1)} copy(bf16[512,3328]{1,0:T(8,128)(2,1)} %get-tuple-element.4) | data formatting | bytes 6815744
  378.6 0.0 copy-done
  378.6 1.0 copy.8
Async XLA Ops:
  374.6 4.0 %copy-start = (bf16[512,1024]{1,0:T(8,128)(2,1)S(1)}, bf16[512,1024]{1,0:T(8,128)(2,1)}, u32[]{:S(2)}) copy-start(bf16[512,1024]{1,0:T(8,128)(2,1)} %get-tuple-element.5) | copy-start | bytes 3145732

commit v2 on v1

--- a/solution.py
+++ b/solution.py
@@ -14,9 +14,11 @@
 MESH = pl.DeviceIdType.MESH
 CHUNKS = 8
 WIDTH = 256
-LAG = 2
+LAGS = 3, 2
 OUT_SLOTS = 3
-AHEAD = 4
+AHEAD = 6
+REST_AT = 2
+HELD = 5
 
 
 def gelu_slope(values):
@@ -45,13 +47,14 @@
         assert self.deep * self.short * CHUNKS == self.count and self.slices * self.width == self.hidden
         self.units = self.chunks * self.slices
         self.far = rows - 1
-        self.lag = LAG if rows <= 4 else 1
         self.ahead = min(AHEAD, self.chunks)
-        self.slope_lag = self.far * self.lag
-        self.down_lag = 2 * self.far * self.lag
+        lags = [m * LAGS[0] // LAGS[1] for m in range(2 * self.far + 1)]
+        self.lags = lags
+        self.slope_lag = lags[self.far]
+        self.down_lag = lags[-1]
         self.hold = self.slope_lag + 1
-        self.in_slots = rows * self.lag + 2
-        self.grad_slots = rows * self.lag + 3
+        self.in_slots = self.slope_lag + 6
+        self.grad_slots = self.down_lag - self.slope_lag + 6
 
     def scratch(self):
         bf, f4 = jnp.bfloat16, jnp.float32
@@ -75,8 +78,8 @@
             x_in=pltpu.VMEM((2, chips, r, low, piece), bf),
             y_out=pltpu.VMEM((chips, r, low, piece), bf),
             y_in=pltpu.VMEM((2, chips, r, low, piece), bf),
-            t_out=pltpu.VMEM((r, low, piece), bf),
-            t_in=pltpu.VMEM((2, r, low, piece), bf),
+            t_out=pltpu.VMEM((n, r, low, piece), bf),
+            t_in=pltpu.VMEM((n, r, low, piece), bf),
             w_sem=dma((self.slices, self.ratio)),
             s1s=dma((n, c)),
             s1r=dma((n, c)),
@@ -96,9 +99,9 @@
             d1r=dma((2, chips)),
             d2s=dma((chips, r)),
             d2r=dma((2, chips, r)),
-            d3s=dma((r,)),
-            d3r=dma((2, r)),
-            d4s=dma((c,)),
+            d3s=dma((n, r)),
+            d3r=dma((n, r)),
+            d4s=dma((n, c)),
             d4r=dma((n, c)),
         )
 
@@ -242,6 +245,8 @@
         stage2(k)
     stage3(0, with_own=False)
     stage4(0)
+    for k in range(pn.ahead, pn.chunks):
+        stage1(k)
 
     def place(v):
         return aligned(v // slices, size), aligned(v % slices, width)
@@ -415,12 +420,12 @@
 
     def row_copy(k, to):
         return remote(
-            b["t_out"].at[to], b["t_in"].at[k % 2, r], b["d3s"].at[to], b["d3r"].at[k % 2, r], (to, c)
+            b["t_out"].at[k, to], b["t_in"].at[k, r], b["d3s"].at[k, to], b["d3r"].at[k, r], (to, c)
         )
 
     def row_arrival(k, source):
         return remote(
-            b["t_out"].at[r], b["t_in"].at[k % 2, source], b["d3s"].at[r], b["d3r"].at[k % 2, source], (source, c)
+            b["t_out"].at[k, r], b["t_in"].at[k, source], b["d3s"].at[k, r], b["d3r"].at[k, source], (source, c)
         )
 
     def owned(k, q):
@@ -433,16 +438,16 @@
         return b["acc"][k % 2, side, rows_of, aligned(down_part, short)]
 
     def owner_copy(k, to, local=False):
-        src = b["t_in"].at[k % 2, to // ratio, :, aligned(to % ratio, thin)]
+        src = b["t_in"].at[k, to // ratio, :, aligned(to % ratio, thin)]
         dst = owned(k, c)
         if local:
-            return pltpu.make_async_copy(src, dst, b["d4s"].at[c])
-        return remote(src, dst, b["d4s"].at[to], b["d4r"].at[k, c], (r, to))
+            return pltpu.make_async_copy(src, dst, b["d4s"].at[k, c])
+        return remote(src, dst, b["d4s"].at[k, to], b["d4r"].at[k, c], (r, to))
 
     def owner_arrival(k, source):
         src = b["t_in"].at[0, 0, :, aligned(0, thin)]
         dst = owned(k, source)
-        return remote(src, dst, b["d4s"].at[source], b["d4r"].at[k, source], (r, source))
+        return remote(src, dst, b["d4s"].at[k, source], b["d4r"].at[k, source], (r, source))
 
     def pair(k):
         for j in list(range(1, chips)) + [0]:
@@ -474,17 +479,7 @@
         others(action, far_first=True)
         action(r)
 
-    def owners_wait():
-        for j in range(1, cols):
-            owner_copy(0, (c + j) % cols).wait_send()
-        owner_copy(0, c, local=True).wait()
-
     def exchange_back(k):
-        @pl.when(k > 0)
-        def _():
-            owners_wait()
-            others(lambda to: row_copy(k, to).wait_send())
-
         def total(row):
             value = acc_part(k, c, row) + b["x_in"][k % 2, 0, row].astype(jnp.float32)
             for j in range(1, chips):
@@ -492,12 +487,18 @@
                 value = value + b["y_in"][k % 2, j, row].astype(jnp.float32)
             return value.astype(jnp.bfloat16)
 
+        send = (k < pn.chunks - HELD) | (k == pn.chunks - 1)
+
         def action(row):
-            b["t_out"][row] = total(row)
-            row_copy(k, row).start()
+            b["t_out"][k, row] = total(row)
+            pl.when(send)(lambda: row_copy(k, row).start())
 
         others(action, far_first=True)
-        b["t_in"][k % 2, r] = total(r)
+        b["t_in"][k, r] = total(r)
+
+    def send_held():
+        for k in range(max(pn.chunks - HELD, 0), pn.chunks - 1):
+            others(lambda to: row_copy(k, to).start(), far_first=True)
 
     def owners(k):
         def action(row):
@@ -529,45 +530,51 @@
 
     og_copy(0).start()
     ends = (0, 1, slices // 3, 2 * slices // 3)
-
-    @pl.loop(0, units + pn.down_lag + ends[-1] + 1)
+    freed = units + pn.lags[2 * far - 1]
+
+    @pl.loop(0, units + pn.down_lag + ends[2] + 1)
     def _(i):
+        def step(m):
+            v = i - pn.lags[m]
+
+            @pl.when(in_range(v))
+            def _():
+                if m < far:
+                    sums(v, m)
+                elif m == far:
+                    slope(v)
+                elif m < 2 * far:
+                    grads(v, m - far)
+                else:
+                    down(v)
+
         @pl.when(i < units)
         def _():
             up(i)
 
-        for h in range(far):
-            v = i - h * pn.lag
-
-            @pl.when(in_range(v))
-            def _(v=v, h=h):
-                sums(v, h)
-
-        @pl.when(in_range(i - pn.slope_lag))
-        def _():
-            slope(i - pn.slope_lag)
-
-        for h in range(1, far):
-            v = i - pn.slope_lag - h * pn.lag
-
-            @pl.when(in_range(v))
-            def _(v=v, h=h):
-                grads(v, h)
-
-        @pl.when(in_range(i - pn.down_lag))
-        def _():
-            down(i - pn.down_lag)
-
-        for lag, action in zip(ends, (pair, plane, exchange_back, owners)):
+        for half in (0, 1):
+            for m in range(half, 2 * far + 1, 2):
+                step(m)
+
+        pl.when(i == freed)(send_held)
+
+        def early_owners(k):
+            pl.when(k < pn.chunks - HELD)(lambda: owners(k))
+
+        for lag, action in zip(ends, (pair, plane, exchange_back, early_owners)):
             at_chunk_end(i - pn.down_lag - lag, action)
 
-        for at, (action, early) in enumerate(
-            ((stage1, pn.ahead), (stage2, pn.ahead), (stage3, 1), (stage4, 1))
-        ):
-
-            @pl.when((i < units - early * slices) & (i % slices == at * slices // 4))
-            def _(action=action, early=early):
-                action(i // slices + early)
+        rest = i - REST_AT
+
+        @pl.when((rest >= 0) & (rest < pn.chunks - pn.ahead))
+        def _():
+            stage2(rest + pn.ahead)
+
+        for at, action in ((2, stage3), (3, stage4)):
+
+            @pl.when((i < units - slices) & (i % slices == at * slices // 4))
+            def _(action=action):
+                action(i // slices + 1)
 
     for back in range(1, OUT_SLOTS + 1):
         for way in (0, 1):
@@ -576,6 +583,10 @@
                 @pl.when(towards(way) <= h)
                 def _(back=back, way=way, h=h):
                     sum_copy(units - back, way, h).wait_send()
+
+    @pl.loop(max(pn.chunks - HELD, 0), pn.chunks)
+    def _(k):
+        owners(k)
 
     for v in (units - 2, units - 1):
         pre_copy(v).wait()
@@ -585,13 +596,14 @@
     for j in range(1, chips):
         for row in range(rows):
             plane_copy(last, j, row).wait_send()
-    others(lambda to: row_copy(last, to).wait_send())
-    owners_wait()
 
     @pl.loop(0, pn.chunks)
     def _(k):
+        others(lambda to: row_copy(k, to).wait_send())
+        owner_copy(k, c, local=True).wait()
         for j in range(1, cols):
             owner_arrival(k, (c + j) % cols).wait_recv()
+            owner_copy(k, (c + j) % cols).wait_send()
 
 
 def per_device(rows, cols, tokens, weight, out_grad):

time: 380 us -> 374 us (0.984)
  Pallas kernels: 374 us -> 368 us
    pallas_call x1, Pallas kernels: 374 us -> 368 us  [per_device(): pl.pallas_call(functools.partial(body, pn, tuple(scratch)), out_shape=(ja...]
where the time goes in v2:
time: 374 us
  Pallas kernels  368 us (98%)
  local copies, waits for them, and re-layouts  4.99 us (1%)
    pallas_call x1, Pallas kernels, per_device(): pl.pallas_call(functools.partial(body, pn, tuple(scratch)), out_shape=(ja...  368 us

profile of v2, /device:TPU:0, one launch (start us, length us, event | category | flops | bytes accessed | tf_op | source)
XLA Modules:
  0.0 373.5 jit_solution(7795129997217467434)
XLA Ops:
  0.6 367.9 %shard_map.50 = (bf16[512,3328]{1,0:T(8,128)(2,1)}, bf16[512,1024]{1,0:T(8,128)(2,1)}) custom-call(bf16[512,1024]{1,0:T(8,128)(2,1)} %tokens.1, bf16[2,8,128,3328]{3,2,1,0:T(8,128)(2,1)} %bitcast.1, bf16[512,3328]{1,0:T(8,128)(2,1)} %out_grad.1), custom_call_target="tpu_custom_call" | custom-call | flops 55834574848 | bytes 13631488 | tf_op jit(solution)/shard_map/pallas_call | solution.py:614
  368.5 0.0 copy-start
  368.5 4.0 %copy.7 = bf16[512,3328]{1,0:T(8,128)(2,1)} copy(bf16[512,3328]{1,0:T(8,128)(2,1)} %get-tuple-element.4) | data formatting | bytes 6815744
  372.6 0.0 copy-done
  372.6 1.0 copy.8
Async XLA Ops:
  368.5 4.0 %copy-start = (bf16[512,1024]{1,0:T(8,128)(2,1)S(1)}, bf16[512,1024]{1,0:T(8,128)(2,1)}, u32[]{:S(2)}) copy-start(bf16[512,1024]{1,0:T(8,128)(2,1)} %get-tuple-element.5) | copy-start | bytes 3145732
